TPU v7x, 32 devices: a whole 2x2x4 slice. The times are simulated.
32 devices in a mesh: groups: 2 (over y), seq: 4 (over z), ep: 2 (over x), tp: 2 (over core).
Axes of the slice: x: 2, y: 2, z: 4, core: 2. Of those that a mesh axis runs over, the one named last changes fastest.
Arguments:
- hidden: bfloat16 [2048, 1440], P(('groups', 'seq', 'ep')), parts along dimension 0, may hold values from -6 to 6
- expert_ids: int32 [2048, 4], P(('groups', 'seq', 'ep')), parts along dimension 0, may hold values from 0 to 7, all different within a row; in each aligned block of 128 rows (0 to 127, 128 to 255, ...) at most 88 rows name the same one
- gate_units: int32 [2048, 4], P(('groups', 'seq', 'ep')), parts along dimension 0, may hold values from 4096 to 32767
- w_gate: bfloat16 [8, 1440, 1440], P(('seq', 'tp'), None, 'ep'), may hold values from -0.15625 to 0.15625
- w_up: bfloat16 [8, 1440, 1440], P(('seq', 'tp'), None, 'ep'), may hold values from -0.15625 to 0.15625
- w_down: bfloat16 [8, 1440, 1440], P(('seq', 'tp'), None, 'ep'), may hold values from -0.15625 to 0.15625
Outputs:
- moe_out: bfloat16 [2048, 1440], P(('groups', 'seq', 'ep'), 'tp'), parts along dimension 0
There are 2 independent parts, one for each index of `groups`. A program takes and returns all parts, laid end to end along the dimension named above; an argument that names none is the same for every part. Nothing has to cross between parts.
Inputs may be any that keep to these rules, and one draw needn't show every extreme that they name: `expert_ids`: each row names 4 different experts; in each aligned block of 128 rows no expert is named by more than 88 rows, and in every draw some expert is named by exactly 88 rows of some block.
All inputs are finite; a program needn't handle non-finite values.
Results may differ from a plain program's by a relative error of at most 0.0064.
Values may be sent and summed in bfloat16 or wider, within the bound.
A program may use at most 64 MiB of HBM per device.

v0:
```python
import jax
import jax.numpy as jnp
from jax import lax
from jax.sharding import PartitionSpec as P

TOP = 4


def slice_output(rows_in, gate_cols, up_cols, down_cols):
    gate_pre = jnp.dot(rows_in, gate_cols, preferred_element_type=jnp.float32)
    up_pre = jnp.dot(rows_in, up_cols, preferred_element_type=jnp.float32)
    activation = ((up_pre + 1.0) * gate_pre * jax.nn.sigmoid(1.702 * gate_pre)).astype(jnp.bfloat16)
    return lax.dot_general(
        activation, down_cols, (((1,), (1,)), ((), ())), preferred_element_type=jnp.float32
    ).astype(jnp.bfloat16)


def local(hidden, expert_ids, gate_units, w_gate, w_up, w_down):
    token_count, model_width = hidden.shape
    seq_count = lax.axis_size("seq")
    ep_count = lax.axis_size("ep")
    tp_count = lax.axis_size("tp")
    half_width = model_width // tp_count
    my_half = lax.axis_index("tp")
    expert_count = seq_count * tp_count
    capacity = max(2, (token_count * TOP * 11 + expert_count * 8 - 1) // (expert_count * 8))
    flat_ids = expert_ids.reshape(-1)
    onehot_ids = (flat_ids[:, None] == jnp.arange(expert_count, dtype=jnp.int32)[None, :]).astype(
        jnp.int32
    )
    slot_rank = jnp.sum((jnp.cumsum(onehot_ids, axis=0) - 1) * onehot_ids, axis=1)
    owner_seq = flat_ids // tp_count
    owner_half = flat_ids % tp_count
    send_row = jnp.where(owner_half == my_half, owner_seq * capacity + slot_rank, -1)
    selector = jnp.arange(seq_count * capacity, dtype=jnp.int32)[:, None] == send_row[None, :]
    selector = jnp.any(selector.reshape(seq_count * capacity, token_count, TOP), axis=2).astype(
        jnp.bfloat16
    )
    outgoing = jnp.dot(selector, hidden, preferred_element_type=jnp.float32).astype(jnp.bfloat16)
    outgoing = outgoing.reshape(seq_count, capacity, model_width)
    column_of = (owner_half * seq_count + owner_seq) * capacity + slot_rank
    gate_share = gate_units.reshape(-1).astype(jnp.float32) / 65536.0
    column_ids = jnp.arange(tp_count * seq_count * capacity, dtype=jnp.int32)
    combiner = jnp.where(column_ids[None, :] == column_of[:, None], gate_share[:, None], 0.0)
    combiner = jnp.sum(combiner.reshape(token_count, TOP, -1), axis=1)
    copied = jnp.broadcast_to(outgoing[:, None], (seq_count, ep_count, capacity, model_width))
    copied = copied.reshape(seq_count * ep_count, capacity, model_width)
    arrived = lax.all_to_all(copied, ("seq", "ep"), split_axis=0, concat_axis=0, tiled=True)
    slice_rows = slice_output(arrived.reshape(-1, model_width), w_gate[0], w_up[0], w_down[0])
    slice_rows = slice_rows.reshape(seq_count * ep_count, capacity, model_width)
    came_back = lax.all_to_all(
        lax.all_to_all(slice_rows, ("seq", "ep"), split_axis=0, concat_axis=0, tiled=True),
        "tp",
        split_axis=2,
        concat_axis=0,
        tiled=True,
    )
    came_back = came_back.reshape(tp_count, seq_count, ep_count, capacity, half_width)
    returned = jnp.sum(came_back.astype(jnp.float32), axis=2).astype(jnp.bfloat16)
    result_rows = returned.reshape(-1, half_width).astype(jnp.float32)
    moe_out = jnp.dot(
        combiner, result_rows, precision=lax.Precision.HIGHEST, preferred_element_type=jnp.float32
    )
    return moe_out.astype(jnp.bfloat16)


def solution(mesh):
    return jax.shard_map(
        local,
        mesh=mesh,
        in_specs=(
            P(("groups", "seq", "ep"), None),
            P(("groups", "seq", "ep"), None),
            P(("groups", "seq", "ep"), None),
            P(("seq", "tp"), None, "ep"),
            P(("seq", "tp"), None, "ep"),
            P(("seq", "tp"), None, "ep"),
        ),
        out_specs=P(("groups", "seq", "ep"), "tp"),
        check_vma=False,
    )
```

profile of v0, /device:TPU:0, one launch (start us, length us, event | category | flops | bytes accessed | tf_op | source)
XLA Modules:
  0.0 157.3 jit_solution(9115896044357004231)
XLA Ops:
  0.0 0.0 copy-start
  0.0 0.9 copy.72
  0.9 0.1 eq.70
  1.0 0.1 eq.66
  1.2 1.1 reduce-window.6
  2.3 0.2 slice_reduce_fusion
  2.6 0.1 fusion.10
  2.7 0.1 reduce_sum.33
  2.8 0.1 copy.74
  2.8 0.7 add_select_fusion.2
  3.6 0.1 fusion.9
  3.7 1.4 convolution_convert_fusion.1
  5.1 0.2 broadcast_in_dim.30
  5.3 0.0 copy-start.3
  5.3 57.4 %all_to_all.25 = bf16[8,88,1440]{2,1,0:T(8,128)(2,1)S(1)} all-to-all(bf16[8,88,1440]{2,1,0:T(8,128)(2,1)S(1)} %bitcast.36), channel_id=1, replica_groups=mesh['groups'=2,'seq'=4,'ep'=2,'tp'=2] {'seq','ep'}, dimensions={0} | all-to-all | bytes 4055040 | tf_op jit(solution)/shard_map/all_to_all | solution.py:48
  62.7 0.0 copy-start.1
  62.7 1.3 copy-done.1
  64.1 0.0 copy-done.3
  64.1 3.2 %fusion.1 = f32[704,720]{1,0:T(8,128)} fusion(bf16[704,1440]{1,0:T(8,128)(2,1)S(1)} %bitcast.40, bf16[1,1440,720]{2,1,0:T(8,128)(2,1)S(1)} %copy-done.3), kind=kOutput, calls=%fused_computation.3 | convolution fusion | flops 1459814400 | bytes 6128640 | tf_op jit(solution)/shard_map/dot_general | solution.py:10
  67.2 0.0 copy-done
  67.2 8.6 %convolution_convert_fusion = bf16[704,1440]{1,0:T(8,128)(2,1)} fusion(bf16[1,1440,720]{2,1,0:T(8,128)(2,1)S(1)} %copy-done, f32[704,720]{1,0:T(8,128)} %fusion.1, bf16[704,1440]{1,0:T(8,128)(2,1)} %bitcast.41, bf16[1,1440,720]{2,1,0:T(8,128)(2,1)} %param.10), kind=kOutput, calls=%fused_computation | convolution fusion | flops 2924697600 | bytes 10229760 | tf_op jit(solution)/shard_map/dot_general | solution.py:13
  75.8 0.0 copy-start.2
  75.8 4.5 %all-to-all-start.1 = ((bf16[8,88,1440]{2,1,0:T(8,128)(2,1)}), bf16[8,88,1440]{2,1,0:T(8,128)(2,1)}, u32[]{:S(2)}, u32[]{:S(2)}) async-start(bf16[8,88,1440]{2,1,0:T(8,128)(2,1)} %bitcast.39), calls=%async_computation.1 | async-start | bytes 4325376 | tf_op jit(solution)/shard_map/all_to_all | solution.py:52
  80.3 0.0 copy-done.2
  80.3 0.2 select_reduce_fusion
  80.5 48.5 %all-to-all-done.1 = bf16[8,88,1440]{2,1,0:T(8,128)(2,1)} async-done(((bf16[8,88,1440]{2,1,0:T(8,128)(2,1)}), bf16[8,88,1440]{2,1,0:T(8,128)(2,1)}, u32[]{:S(2)}, u32[]{:S(2)}) %all-to-all-start.1) | async-done | bytes 2027552 | tf_op jit(solution)/shard_map/all_to_all | solution.py:52
  129.0 4.7 %copy.76 = bf16[8,88,1440]{1,0,2:T(8,128)(2,1)} copy(bf16[8,88,1440]{2,1,0:T(8,128)(2,1)} %all-to-all-done.1) | data formatting | bytes 4055040 | tf_op jit(solution)/shard_map/all_to_all | solution.py:52
  133.8 10.1 %all_to_all.26 = bf16[8,88,1440]{1,0,2:T(8,128)(2,1)} all-to-all(bf16[8,88,1440]{1,0,2:T(8,128)(2,1)} %copy.76), channel_id=1, replica_groups=mesh['groups'=2,'seq'=4,'ep'=2,'tp'=2] {'tp'}, dimensions={2} | all-to-all | bytes 4055040 | tf_op jit(solution)/shard_map/all_to_all | solution.py:51
  143.8 6.2 %copy.77 = bf16[2,8,88,720]{3,0,2,1:T(2,128)(2,1)} copy(bf16[2,8,88,720]{2,1,3,0:T(8,128)(2,1)} %bitcast.35) | data formatting | bytes 4055040 | tf_op jit(solution)/shard_map/all_to_all | solution.py:51
  150.0 5.2 %bitcast_reduce_fusion = bf16[2,4,88,720]{3,0,2,1:T(2,128)(2,1)S(1)} fusion(bf16[2,8,88,720]{3,0,2,1:T(2,128)(2,1)} %copy.77), kind=kLoop, calls=%fused_computation.7 | loop fusion | flops 506880 | bytes 3041280 | tf_op jit(solution)/shard_map/reduce_sum | solution.py:59
  155.2 0.1 copy.78
  155.3 2.0 %convolution_convert_fusion.2 = bf16[128,720]{0,1:T(8,128)(2,1)} fusion(f32[128,704]{0,1:T(8,128)S(1)} %select_reduce_fusion, bf16[704,720]{1,0:T(8,128)(2,1)S(1)} %bitcast.37), kind=kOutput, calls=%fused_computation.11 | convolution fusion | flops 778659840 | bytes 1558528 | tf_op jit(solution)/shard_map/dot_general | solution.py:61
  (4 shorter events, 0.0 us)
Async XLA Ops:
  0.0 67.2 %copy-start = (bf16[1,1440,720]{2,1,0:T(8,128)(2,1)S(1)}, bf16[1,1440,720]{2,1,0:T(8,128)(2,1)}, u32[]{:S(2)}) copy-start(bf16[1,1440,720]{2,1,0:T(8,128)(2,1)} %param.11) | copy-start | bytes 6220804
  5.3 58.8 %copy-start.3 = (bf16[1,1440,720]{2,1,0:T(8,128)(2,1)S(1)}, bf16[1,1440,720]{2,1,0:T(8,128)(2,1)}, u32[]{:S(2)}) copy-start(bf16[1,1440,720]{2,1,0:T(8,128)(2,1)} %param.9) | copy-start | bytes 6220804
  62.7 1.3 copy-start.1
  75.8 4.5 %copy-start.2 = (s32[128,4]{0,1:T(4,128)S(1)}, s32[128,4]{0,1:T(4,128)}, u32[]{:S(2)}) copy-start(s32[128,4]{0,1:T(4,128)} %param.8) | copy-start | bytes 6148
  75.8 53.2 %all-to-all-start.1 = ((bf16[8,88,1440]{2,1,0:T(8,128)(2,1)}), bf16[8,88,1440]{2,1,0:T(8,128)(2,1)}, u32[]{:S(2)}, u32[]{:S(2)}) async-start(bf16[8,88,1440]{2,1,0:T(8,128)(2,1)} %bitcast.39), calls=%async_computation.1 | async-start | bytes 4325376 | tf_op jit(solution)/shard_map/all_to_all | solution.py:52
where the time goes:
time: 158 us; the launch traced here: 157 us
  blocking collectives  67.5 us (43%)
  waiting for transfers between devices  48.5 us (31%)
  matrix products  15.2 us (10%)
  local copies, waits for them, and re-layouts  14.1 us (9%)
  other arithmetic  7.45 us (5%)
  starting transfers between devices  4.5 us (3%)
    all_to_all x1, blocking collectives, local(): lax.all_to_all(copied, ('seq', 'ep'), split_axis=0, concat_axis=0, tiled=...  57.4 us
    all_to_all x1, waiting for transfers between devices, local(): lax.all_to_all(slice_rows, ('seq', 'ep'), split_axis=0, concat_axis=0, ti...  48.5 us
    all_to_all x1, blocking collectives, local(): lax.all_to_all(lax.all_to_all(slice_rows, ('seq', 'ep'), split_axis=0, co...  10.1 us
    dot_general x1, matrix products, slice_output(): lax.dot_general(activation, down_cols, (((1,), (1,)), ((), ())), preferre...  8.55 us
    all_to_all x1, local copies, waits for them, and re-layouts, local(): lax.all_to_all(lax.all_to_all(slice_rows, ('seq', 'ep'), split_axis=0, co...  6.16 us
    reduce_sum x1, other arithmetic, local(): jnp.sum(came_back.astype(jnp.float32), axis=2).astype(jnp.bfloat16)  5.2 us
    all_to_all x1, local copies, waits for them, and re-layouts, local(): lax.all_to_all(slice_rows, ('seq', 'ep'), split_axis=0, concat_axis=0, ti...  4.73 us
    all_to_all x1, starting transfers between devices, local(): lax.all_to_all(slice_rows, ('seq', 'ep'), split_axis=0, concat_axis=0, ti...  4.5 us
  transfers between devices with their start and end apart: 1, of which 1 were waited for; matrix products, arithmetic and copies ran while one was open for 0% of the time, Pallas kernels for 0%

commit v1 on v0

--- a/solution.py
+++ b/solution.py
@@ -4,6 +4,22 @@
 from jax.sharding import PartitionSpec as P
 
 TOP = 4
+
+
+def pairwise_exchange(x, axis, split, join):
+    ways, here = (lax.axis_size(axis), lax.axis_index(axis))
+    width = x.shape[split] // ways
+    lengths = list(x.shape)
+    lengths[split] = width
+    height = lengths[join]
+    lengths[join] = height * ways
+    full = jnp.zeros(lengths, x.dtype)
+    for mask in range(ways):
+        part = lax.dynamic_slice_in_dim(x, (here ^ mask) * width, width, axis=split)
+        if mask:
+            part = lax.ppermute(part, axis, [(d, d ^ mask) for d in range(ways)])
+        full = lax.dynamic_update_slice_in_dim(full, part, (here ^ mask) * height, axis=join)
+    return full
 
 
 def slice_output(rows_in, gate_cols, up_cols, down_cols):
@@ -45,7 +61,7 @@
     combiner = jnp.sum(combiner.reshape(token_count, TOP, -1), axis=1)
     copied = jnp.broadcast_to(outgoing[:, None], (seq_count, ep_count, capacity, model_width))
     copied = copied.reshape(seq_count * ep_count, capacity, model_width)
-    arrived = lax.all_to_all(copied, ("seq", "ep"), split_axis=0, concat_axis=0, tiled=True)
+    arrived = pairwise_exchange(copied, ("seq", "ep"), 0, 0)
     slice_rows = slice_output(arrived.reshape(-1, model_width), w_gate[0], w_up[0], w_down[0])
     slice_rows = slice_rows.reshape(seq_count * ep_count, capacity, model_width)
     came_back = lax.all_to_all(

time: 158 us -> 156 us (0.987)
  blocking collectives: 67.5 us -> 10.1 us
  waiting for transfers between devices: 48.5 us -> 80.1 us
  starting transfers between devices: 4.5 us -> 27.5 us
    all_to_all x1 -> x0, blocking collectives: 57.4 us -> none  [local(): lax.all_to_all(copied, ('seq', 'ep'), split_axis=0, concat_axis=0, tiled=...]
    ppermute x0 -> x7, waiting for transfers between devices: none -> 31.3 us  [pairwise_exchange(): part = lax.ppermute(part, axis, [(d, d ^ mask) for d in range(ways)])]
    ppermute x0 -> x7, starting transfers between devices: none -> 13.8 us  [pairwise_exchange(): part = lax.ppermute(part, axis, [(d, d ^ mask) for d in range(ways)])]
    all_to_all x1, starting transfers between devices: 4.5 us -> 13.7 us  [local(): lax.all_to_all(slice_rows, ('seq', 'ep'), split_axis=0, concat_axis=0, ti...]
  transfers between devices with their start and end apart: 1 -> 8, of which waited for: 1 -> 5; matrix products, arithmetic and copies ran while one was open for 0% -> 0% of each run, Pallas kernels for 0% -> 0%
where the time goes in v1:
time: 156 us; the launch traced here: 155 us
  waiting for transfers between devices  80.1 us (51%)
  starting transfers between devices  27.5 us (18%)
  matrix products  15.2 us (10%)
  local copies, waits for them, and re-layouts  14.5 us (9%)
  blocking collectives  10.1 us (6%)
  other arithmetic  7.45 us (5%)
    all_to_all x1, waiting for transfers between devices, local(): lax.all_to_all(slice_rows, ('seq', 'ep'), split_axis=0, concat_axis=0, ti...  48.8 us
    ppermute x7, waiting for transfers between devices, pairwise_exchange(): part = lax.ppermute(part, axis, [(d, d ^ mask) for d in range(ways)])  31.3 us
    ppermute x7, starting transfers between devices, pairwise_exchange(): part = lax.ppermute(part, axis, [(d, d ^ mask) for d in range(ways)])  13.8 us
    all_to_all x1, starting transfers between devices, local(): lax.all_to_all(slice_rows, ('seq', 'ep'), split_axis=0, concat_axis=0, ti...  13.7 us
    all_to_all x1, blocking collectives, local(): lax.all_to_all(lax.all_to_all(slice_rows, ('seq', 'ep'), split_axis=0, co...  10.1 us
    dot_general x1, matrix products, slice_output(): lax.dot_general(activation, down_cols, (((1,), (1,)), ((), ())), preferre...  8.59 us
    all_to_all x1, local copies, waits for them, and re-layouts, local(): lax.all_to_all(lax.all_to_all(slice_rows, ('seq', 'ep'), split_axis=0, co...  6.16 us
    reduce_sum x1, other arithmetic, local(): jnp.sum(came_back.astype(jnp.float32), axis=2).astype(jnp.bfloat16)  5.2 us
  transfers between devices with their start and end apart: 8, of which 5 were waited for; matrix products, arithmetic and copies ran while one was open for 0% of the time, Pallas kernels for 0%

profile of v1, /device:TPU:0, one launch (start us, length us, event | category | flops | bytes accessed | tf_op | source)
XLA Modules:
  0.0 155.1 jit_solution(8149848130515577488)
XLA Ops:
  0.0 0.9 copy.72
  1.0 0.1 eq.66
  1.2 1.1 reduce-window.6
  2.3 0.2 slice_reduce_fusion
  2.7 0.1 reduce_sum.33
  2.8 0.7 add_select_fusion.2
  3.7 1.4 convolution_convert_fusion.1
  5.1 0.2 broadcast_in_dim.34
  5.3 0.1 broadcast_in_dim.32
  5.5 0.2 constant_dynamic-slice_fusion
  5.7 3.0 %collective-permute-start = (bf16[1,88,1440]{2,1,0:T(8,128)(2,1)S(1)}, bf16[1,88,1440]{2,1,0:T(8,128)(2,1)S(1)}, u32[]{:S(2)}, u32[]{:S(2)}) collective-permute-start(bf16[1,88,1440]{2,1,0:T(8,128)(2,1)S(1)} %get-tuple-element.11), channel_id=1, source_target_pairs={{0,2},{2,0},{4,6},{6,4},{8,10},{10,8},{12,14},{14,12},{1,3},{3,1},... | collective-permute-start | bytes 760328 | tf_op jit(solution)/shard_map/ppermute | solution.py:20
  8.7 1.6 %collective-permute-start.1 = (bf16[1,88,1440]{2,1,0:T(8,128)(2,1)S(1)}, bf16[1,88,1440]{2,1,0:T(8,128)(2,1)S(1)}, u32[]{:S(2)}, u32[]{:S(2)}) collective-permute-start(bf16[1,88,1440]{2,1,0:T(8,128)(2,1)S(1)} %get-tuple-element.10), channel_id=1, source_target_pairs={{0,4},{2,6},{4,0},{6,2},{8,12},{10,14},{12,8},{14,10},{1,5},{3,7},... | collective-permute-start | bytes 760328 | tf_op jit(solution)/shard_map/ppermute | solution.py:20
  10.3 3.0 %collective-permute-start.3 = (bf16[1,88,1440]{2,1,0:T(8,128)(2,1)S(1)}, bf16[1,88,1440]{2,1,0:T(8,128)(2,1)S(1)}, u32[]{:S(2)}, u32[]{:S(2)}) collective-permute-start(bf16[1,88,1440]{2,1,0:T(8,128)(2,1)S(1)} %get-tuple-element.8), channel_id=1, source_target_pairs={{0,8},{2,10},{4,12},{6,14},{8,0},{10,2},{12,4},{14,6},{1,9},{3,11}... | collective-permute-start | bytes 760328 | tf_op jit(solution)/shard_map/ppermute | solution.py:20
  13.3 1.3 collective-permute-start.4
  14.5 0.6 collective-permute-done
  15.2 3.9 %collective-permute-start.5 = (bf16[1,88,1440]{2,1,0:T(8,128)(2,1)S(1)}, bf16[1,88,1440]{2,1,0:T(8,128)(2,1)S(1)}, u32[]{:S(2)}, u32[]{:S(2)}) collective-permute-start(bf16[1,88,1440]{2,1,0:T(8,128)(2,1)S(1)} %get-tuple-element.6), channel_id=1, source_target_pairs={{0,12},{2,14},{4,8},{6,10},{8,4},{10,6},{12,0},{14,2},{1,13},{3,15... | collective-permute-start | bytes 760328 | tf_op jit(solution)/shard_map/ppermute | solution.py:20
  19.1 9.7 %collective-permute-done.1 = bf16[1,88,1440]{2,1,0:T(8,128)(2,1)S(1)} collective-permute-done((bf16[1,88,1440]{2,1,0:T(8,128)(2,1)S(1)}, bf16[1,88,1440]{2,1,0:T(8,128)(2,1)S(1)}, u32[]{:S(2)}, u32[]{:S(2)}) %collective-permute-start.1) | collective-permute-done | bytes 253472 | tf_op jit(solution)/shard_map/ppermute | solution.py:20
  28.7 1.1 collective-permute-start.6
  29.8 2.5 %collective-permute-done.2 = bf16[1,88,1440]{2,1,0:T(8,128)(2,1)S(1)} collective-permute-done((bf16[1,88,1440]{2,1,0:T(8,128)(2,1)S(1)}, bf16[1,88,1440]{2,1,0:T(8,128)(2,1)S(1)}, u32[]{:S(2)}, u32[]{:S(2)}) %collective-permute-start.2) | collective-permute-done | bytes 253472 | tf_op jit(solution)/shard_map/ppermute | solution.py:20
  32.3 18.5 %collective-permute-done.4 = bf16[1,88,1440]{2,1,0:T(8,128)(2,1)S(1)} collective-permute-done((bf16[1,88,1440]{2,1,0:T(8,128)(2,1)S(1)}, bf16[1,88,1440]{2,1,0:T(8,128)(2,1)S(1)}, u32[]{:S(2)}, u32[]{:S(2)}) %collective-permute-start.4) | collective-permute-done | bytes 253472 | tf_op jit(solution)/shard_map/ppermute | solution.py:20
  51.0 1.3 copy-done.1
  52.3 3.2 %fusion.3 = f32[704,720]{1,0:T(8,128)} fusion(bf16[704,1440]{1,0:T(8,128)(2,1)S(1)} %bitcast.39, bf16[1,1440,720]{2,1,0:T(8,128)(2,1)S(1)} %copy-done.3), kind=kOutput, calls=%fused_computation.5 | convolution fusion | flops 1459814400 | bytes 6128640 | tf_op jit(solution)/shard_map/dot_general | solution.py:27
  55.5 8.6 %convolution_convert_fusion = bf16[704,1440]{1,0:T(8,128)(2,1)} fusion(bf16[1,1440,720]{2,1,0:T(8,128)(2,1)S(1)} %copy-done, f32[704,720]{1,0:T(8,128)} %fusion.3, bf16[704,1440]{1,0:T(8,128)(2,1)} %bitcast.40, bf16[1,1440,720]{2,1,0:T(8,128)(2,1)} %param.9), kind=kOutput, calls=%fused_computation | convolution fusion | flops 2924697600 | bytes 10229760 | tf_op jit(solution)/shard_map/dot_general | solution.py:29
  64.1 13.7 %all-to-all-start = ((bf16[8,88,1440]{2,1,0:T(8,128)(2,1)}), bf16[8,88,1440]{2,1,0:T(8,128)(2,1)}, u32[]{:S(2)}, u32[]{:S(2)}) async-start(bf16[8,88,1440]{2,1,0:T(8,128)(2,1)} %bitcast.41), calls=%async_computation | async-start | bytes 4325376 | tf_op jit(solution)/shard_map/all_to_all | solution.py:68
  77.8 0.2 select_reduce_fusion
  77.9 48.8 %all-to-all-done = bf16[8,88,1440]{2,1,0:T(8,128)(2,1)} async-done(((bf16[8,88,1440]{2,1,0:T(8,128)(2,1)}), bf16[8,88,1440]{2,1,0:T(8,128)(2,1)}, u32[]{:S(2)}, u32[]{:S(2)}) %all-to-all-start) | async-done | bytes 2027552 | tf_op jit(solution)/shard_map/all_to_all | solution.py:68
  126.8 4.7 %copy.76 = bf16[8,88,1440]{1,0,2:T(8,128)(2,1)} copy(bf16[8,88,1440]{2,1,0:T(8,128)(2,1)} %all-to-all-done) | data formatting | bytes 4055040 | tf_op jit(solution)/shard_map/all_to_all | solution.py:68
  131.5 10.1 %all_to_all.20 = bf16[8,88,1440]{1,0,2:T(8,128)(2,1)} all-to-all(bf16[8,88,1440]{1,0,2:T(8,128)(2,1)} %copy.76), channel_id=1, replica_groups=mesh['groups'=2,'seq'=4,'ep'=2,'tp'=2] {'tp'}, dimensions={2} | all-to-all | bytes 4055040 | tf_op jit(solution)/shard_map/all_to_all | solution.py:67
  141.5 6.2 %copy.77 = bf16[2,8,88,720]{3,0,2,1:T(2,128)(2,1)} copy(bf16[2,8,88,720]{2,1,3,0:T(8,128)(2,1)} %bitcast.35) | data formatting | bytes 4055040 | tf_op jit(solution)/shard_map/all_to_all | solution.py:67
  147.7 5.2 %bitcast_reduce_fusion = bf16[2,4,88,720]{3,0,2,1:T(2,128)(2,1)S(1)} fusion(bf16[2,8,88,720]{3,0,2,1:T(2,128)(2,1)} %copy.77), kind=kLoop, calls=%fused_computation.7 | loop fusion | flops 506880 | bytes 3041280 | tf_op jit(solution)/shard_map/reduce_sum | solution.py:75
  152.9 0.1 copy.78
  153.0 2.0 %convolution_convert_fusion.2 = bf16[128,720]{0,1:T(8,128)(2,1)} fusion(f32[128,704]{0,1:T(8,128)S(1)} %select_reduce_fusion, bf16[704,720]{1,0:T(8,128)(2,1)S(1)} %bitcast.37), kind=kOutput, calls=%fused_computation.11 | convolution fusion | flops 778659840 | bytes 1558528 | tf_op jit(solution)/shard_map/dot_general | solution.py:77
  (26 shorter events, 0.6 us)
Async XLA Ops:
  0.0 55.5 %copy-start = (bf16[1,1440,720]{2,1,0:T(8,128)(2,1)S(1)}, bf16[1,1440,720]{2,1,0:T(8,128)(2,1)}, u32[]{:S(2)}) copy-start(bf16[1,1440,720]{2,1,0:T(8,128)(2,1)} %param.11) | copy-start | bytes 6220804
  5.7 46.6 %copy-start.3 = (bf16[1,1440,720]{2,1,0:T(8,128)(2,1)S(1)}, bf16[1,1440,720]{2,1,0:T(8,128)(2,1)}, u32[]{:S(2)}) copy-start(bf16[1,1440,720]{2,1,0:T(8,128)(2,1)} %param.10) | copy-start | bytes 6220804
  5.7 9.5 %collective-permute-start = (bf16[1,88,1440]{2,1,0:T(8,128)(2,1)S(1)}, bf16[1,88,1440]{2,1,0:T(8,128)(2,1)S(1)}, u32[]{:S(2)}, u32[]{:S(2)}) collective-permute-start(bf16[1,88,1440]{2,1,0:T(8,128)(2,1)S(1)} %get-tuple-element.11), channel_id=1, source_target_pairs={{0,2},{2,0},{4,6},{6,4},{8,10},{10,8},{12,14},{14,12},{1,3},{3,1},... | collective-permute-start | bytes 760328 | tf_op jit(solution)/shard_map/ppermute | solution.py:20
  8.7 20.0 %collective-permute-start.1 = (bf16[1,88,1440]{2,1,0:T(8,128)(2,1)S(1)}, bf16[1,88,1440]{2,1,0:T(8,128)(2,1)S(1)}, u32[]{:S(2)}, u32[]{:S(2)}) collective-permute-start(bf16[1,88,1440]{2,1,0:T(8,128)(2,1)S(1)} %get-tuple-element.10), channel_id=1, source_target_pairs={{0,4},{2,6},{4,0},{6,2},{8,12},{10,14},{12,8},{14,10},{1,5},{3,7},... | collective-permute-start | bytes 760328 | tf_op jit(solution)/shard_map/ppermute | solution.py:20
  10.3 22.0 %collective-permute-start.2 = (bf16[1,88,1440]{2,1,0:T(8,128)(2,1)S(1)}, bf16[1,88,1440]{2,1,0:T(8,128)(2,1)S(1)}, u32[]{:S(2)}, u32[]{:S(2)}) collective-permute-start(bf16[1,88,1440]{2,1,0:T(8,128)(2,1)S(1)} %get-tuple-element.9), channel_id=1, source_target_pairs={{0,6},{2,4},{4,2},{6,0},{8,14},{10,12},{12,10},{14,8},{1,7},{3,5},... | collective-permute-start | bytes 760328 | tf_op jit(solution)/shard_map/ppermute | solution.py:20
  10.3 22.0 %collective-permute-start.3 = (bf16[1,88,1440]{2,1,0:T(8,128)(2,1)S(1)}, bf16[1,88,1440]{2,1,0:T(8,128)(2,1)S(1)}, u32[]{:S(2)}, u32[]{:S(2)}) collective-permute-start(bf16[1,88,1440]{2,1,0:T(8,128)(2,1)S(1)} %get-tuple-element.8), channel_id=1, source_target_pairs={{0,8},{2,10},{4,12},{6,14},{8,0},{10,2},{12,4},{14,6},{1,9},{3,11}... | collective-permute-start | bytes 760328 | tf_op jit(solution)/shard_map/ppermute | solution.py:20
  13.3 37.5 %collective-permute-start.4 = (bf16[1,88,1440]{2,1,0:T(8,128)(2,1)S(1)}, bf16[1,88,1440]{2,1,0:T(8,128)(2,1)S(1)}, u32[]{:S(2)}, u32[]{:S(2)}) collective-permute-start(bf16[1,88,1440]{2,1,0:T(8,128)(2,1)S(1)} %get-tuple-element.7), channel_id=1, source_target_pairs={{0,10},{2,8},{4,14},{6,12},{8,2},{10,0},{12,6},{14,4},{1,11},{3,9}... | collective-permute-start | bytes 760328 | tf_op jit(solution)/shard_map/ppermute | solution.py:20
  15.2 35.7 %collective-permute-start.5 = (bf16[1,88,1440]{2,1,0:T(8,128)(2,1)S(1)}, bf16[1,88,1440]{2,1,0:T(8,128)(2,1)S(1)}, u32[]{:S(2)}, u32[]{:S(2)}) collective-permute-start(bf16[1,88,1440]{2,1,0:T(8,128)(2,1)S(1)} %get-tuple-element.6), channel_id=1, source_target_pairs={{0,12},{2,14},{4,8},{6,10},{8,4},{10,6},{12,0},{14,2},{1,13},{3,15... | collective-permute-start | bytes 760328 | tf_op jit(solution)/shard_map/ppermute | solution.py:20
  28.7 22.2 %collective-permute-start.6 = (bf16[1,88,1440]{2,1,0:T(8,128)(2,1)S(1)}, bf16[1,88,1440]{2,1,0:T(8,128)(2,1)S(1)}, u32[]{:S(2)}, u32[]{:S(2)}) collective-permute-start(bf16[1,88,1440]{2,1,0:T(8,128)(2,1)S(1)} %get-tuple-element.5), channel_id=1, source_target_pairs={{0,14},{2,12},{4,10},{6,8},{8,6},{10,4},{12,2},{14,0},{1,15},{3,13... | collective-permute-start | bytes 760328 | tf_op jit(solution)/shard_map/ppermute | solution.py:20
  51.0 1.3 copy-start.1
  64.1 13.7 %copy-start.2 = (s32[128,4]{0,1:T(4,128)S(1)}, s32[128,4]{0,1:T(4,128)}, u32[]{:S(2)}) copy-start(s32[128,4]{0,1:T(4,128)} %param.8) | copy-start | bytes 6148
  64.1 62.7 %all-to-all-start = ((bf16[8,88,1440]{2,1,0:T(8,128)(2,1)}), bf16[8,88,1440]{2,1,0:T(8,128)(2,1)}, u32[]{:S(2)}, u32[]{:S(2)}) async-start(bf16[8,88,1440]{2,1,0:T(8,128)(2,1)} %bitcast.41), calls=%async_computation | async-start | bytes 4325376 | tf_op jit(solution)/shard_map/all_to_all | solution.py:68
